TPU v7x, 256 devices: a whole 4x4x8 slice. The times are simulated.
256 devices in a mesh: seq: 32 (over y, z_lo, core), head: 8 (over x, z_hi).
Axes of the slice: x: 4, y: 4, z: 8 (z_hi: 2, z_lo: 4; z = z_hi * 4 + z_lo), core: 2. Of those that a mesh axis runs over, the one named last changes fastest.
Arguments:
- tokens: bfloat16 [131072, 1024], P(('seq', 'head')), may hold values from -32 to 32
- w_qkv: bfloat16 [1024, 3072], P('seq'), may hold values from -0.1875 to 0.1875
- w_out: bfloat16 [1024, 1024], P('seq'), may hold values from -0.1875 to 0.1875
- neighbours: int32 [1024, 12], P('seq'), may hold values from 0 to 1023, as said below
Outputs:
- update: bfloat16 [131072, 1024], P(('seq', 'head'))
Inputs may be any that keep to these rules, and one draw needn't show every extreme that they name: Block b has grid coordinates z = b // 16, y = (b // 4) % 4, x = b % 4. Each row lists b itself first, then 11 different blocks among its 26 neighbours at offsets -1, 0, 1 in each coordinate (z taken modulo 1024 // 16, y and x modulo 4).
All inputs are finite; a program needn't handle non-finite values.
Results may differ from a plain program's by a relative error of at most 0.0065.
The roundings to bfloat16 on the way count: a program that leaves them out, or rounds other values in their place, can miss the bound.
Values may be sent and summed in bfloat16 or wider, within the bound.
A program may use at most 64 MiB of HBM per device.

v0:
```python
import math
import jax
import jax.numpy as jnp
from jax import lax
from jax.sharding import PartitionSpec as P

HEADS = 8
HD = 128
BLK = 128
NBR = 12
PB = 16


def padded_2(cells, sides, width):
    for axis, dim in sides:
        count = lax.axis_size(axis)
        head = lax.slice_in_dim(cells, 0, width, axis=dim)
        tail = lax.slice_in_dim(cells, cells.shape[dim] - width, cells.shape[dim], axis=dim)
        cells = jnp.concatenate(
            [
                lax.ppermute(tail, axis, [(i, (i + 1) % count) for i in range(count)]),
                cells,
                lax.ppermute(head, axis, [((i + 1) % count, i) for i in range(count)]),
            ],
            axis=dim,
        )
    return cells


def local(tokens, w_qkv, w_out, neighbours):
    head_count = lax.axis_size("head")
    seq_count = lax.axis_size("seq")
    per_device = HEADS // head_count
    local_rows = tokens.shape[0]
    slab_rows = local_rows * head_count
    full_qkv = lax.all_gather(w_qkv, "seq", axis=0, tiled=True)
    projected = jnp.dot(tokens, full_qkv, preferred_element_type=jnp.float32)
    projected = projected.astype(jnp.bfloat16).reshape(local_rows, 3, HEADS, HD)
    slab = lax.all_to_all(projected, "head", split_axis=2, concat_axis=0, tiled=True)
    queries = slab[:, 0]
    key_value = slab[:, 1:3]
    padded = padded_2(key_value, (("seq", 0),), PB * BLK)
    kv_blocks = padded.reshape(-1, BLK, 2, per_device, HD)
    block_count = neighbours.shape[0]
    first_block = lax.axis_index("seq") * block_count
    local_lists = jnp.mod(neighbours - first_block + PB, block_count * seq_count)
    group_blocks = 4
    scale = 1.0 / math.sqrt(HD)

    def attend(args):
        query_group, list_group = args
        picked = kv_blocks[list_group].reshape(group_blocks, NBR * BLK, 2, per_device, HD)
        keys = picked[:, :, 0]
        values = picked[:, :, 1]
        scores = (
            jnp.einsum("nqhd,nkhd->nhqk", query_group, keys, preferred_element_type=jnp.float32)
            * scale
        )
        largest = jnp.max(scores, axis=-1, keepdims=True)
        expo = jnp.exp(scores - largest)
        probs = (expo / jnp.sum(expo, axis=-1, keepdims=True)).astype(jnp.bfloat16)
        result = jnp.einsum("nhqk,nkhd->nqhd", probs, values, preferred_element_type=jnp.float32)
        return result.astype(jnp.bfloat16)

    grouped_q = queries.reshape(block_count // group_blocks, group_blocks, BLK, per_device, HD)
    grouped_l = local_lists.reshape(block_count // group_blocks, group_blocks, NBR)
    attended = lax.map(attend, (grouped_q, grouped_l)).reshape(slab_rows, per_device, HD)
    returned = lax.all_to_all(attended, "head", split_axis=0, concat_axis=1, tiled=True)
    flat = returned.reshape(local_rows, HEADS * HD)
    full_out = lax.all_gather(w_out, "seq", axis=0, tiled=True)
    update = jnp.dot(flat, full_out, preferred_element_type=jnp.float32)
    return update.astype(jnp.bfloat16)


def solution(mesh):
    return jax.shard_map(
        local,
        mesh=mesh,
        in_specs=(P(("seq", "head"), None), P("seq", None), P("seq", None), P("seq", None)),
        out_specs=P(("seq", "head"), None),
        check_vma=False,
    )
```

profile of v0, /device:TPU:33, one launch (start us, length us, event | category | flops | bytes accessed | tf_op | source)
XLA Modules:
  0.0 384.4 jit_solution(7192390426923187747)
XLA Ops:
  7.3 71.2 %all-gather.3.cloned.1.call-done = bf16[1024,3072]{1,0:T(8,128)(2,1)} async-done(((bf16[32,3072]{1,0:T(8,128)(2,1)}), bf16[1024,3072]{1,0:T(8,128)(2,1)}) %all-gather.3.cloned.1.call-update) | async-done | bytes 6291472 | tf_op jit(solution)/shard_map/all_gather | solution.py:36
  78.5 6.4 %fusion.29 = bf16[64,8,24,128]{3,1,2,0:T(8,128)(2,1)S(1)} fusion(bf16[512,1024]{1,0:T(8,128)(2,1)S(1)} %copy-done, bf16[1024,3072]{1,0:T(8,128)(2,1)} %all-gather.3.cloned.1.call-done), kind=kOutput, calls=%fused_computation.27 | convolution fusion | flops 3222798336 | bytes 10485760 | tf_op jit(solution)/shard_map/dot_general | solution.py:37
  86.5 82.3 %all_to_all.33 = bf16[512,3,8,128]{3,0,1,2:T(8,128)(2,1)S(1)} all-to-all(bf16[512,3,8,128]{3,0,1,2:T(8,128)(2,1)S(1)} %copy.20), channel_id=1, replica_groups=mesh['seq'=32,'head'=8] {'head'}, dimensions={2} | all-to-all | bytes 6291456 | tf_op jit(solution)/shard_map/all_to_all | solution.py:39
  178.5 16.8 %collective-permute-done = bf16[2048,2,1,128]{3,0,1,2:T(8,128)(2,1)} collective-permute-done((bf16[2048,2,1,128]{3,0,1,2:T(8,128)(2,1)}, bf16[2048,2,1,128]{3,0,1,2:T(8,128)(2,1)}, u32[]{:S(2)}, u32[]{:S(2)}) %collective-permute-start) | collective-permute-done | bytes 1048608 | tf_op jit(solution)/shard_map/ppermute | solution.py:21
  195.2 8.9 %collective-permute-done.1 = bf16[2048,2,1,128]{3,0,1,2:T(8,128)(2,1)} collective-permute-done((bf16[2048,2,1,128]{3,0,1,2:T(8,128)(2,1)S(1)}, bf16[2048,2,1,128]{3,0,1,2:T(8,128)(2,1)}, u32[]{:S(2)}, u32[]{:S(2)}) %collective-permute-start.1) | collective-permute-done | bytes 1048608 | tf_op jit(solution)/shard_map/ppermute | solution.py:23
  208.1 123.6 %while.10 = (s32[]{:T(128)}, bf16[8,4,128,1,128]{4,2,1,0,3:T(8,128)(2,1)S(1)}, s32[8,4,12]{2,1,0:T(4,128)S(1)}, bf16[64,128,2,1,128]{4,1,3,2,0:T(8,128)(2,1)}, bf16[8,4,128,1,128]{4,2,1,3,0:T(8,128)(2,1)}, /*index=5*/s32[]{:T(128)}) while((s32[]{:T(128)}, bf16[8,4,128,1,128]{4,2,1,0,3:T(8,128)(2,1)S(1)}, s32[8,4,12]{2,1,0:T(4,128)S(1)}, ...), condition=%wide.region_3.4_spmd, body=%wide.region_0.3_spmd.sunk | while | flops 609555072 | bytes 18229452 | solution.py:67
  208.2 4.9 %gather_fusion = bf16[48,128,2,128]{3,1,2,0:T(8,128)(2,1)} fusion(bf16[64,128,2,128]{3,1,2,0:T(8,128)(2,1)} %bitcast.87, s32[1024]{0:T(1024)S(1)} %pad_clamp_fusion.2), kind=kCustom, calls=%fused_computation.clone.1 | custom fusion | bytes 6291648 | tf_op jit(solution)/shard_map/while/body/eval_jaxpr/gather | solution.py:52
  213.2 4.0 %copy.35 = bf16[48,128,2,128]{3,1,0,2:T(8,128)(2,1)} copy(bf16[48,128,2,128]{3,1,2,0:T(8,128)(2,1)} %gather_fusion) | data formatting | bytes 6291456 | tf_op jit(solution)/shard_map/while/body/eval_jaxpr/gather | solution.py:52
  223.7 4.9 %gather_fusion = bf16[48,128,2,128]{3,1,2,0:T(8,128)(2,1)} fusion(bf16[64,128,2,128]{3,1,2,0:T(8,128)(2,1)} %bitcast.87, s32[1024]{0:T(1024)S(1)} %pad_clamp_fusion.2), kind=kCustom, calls=%fused_computation.clone.1 | custom fusion | bytes 6291648 | tf_op jit(solution)/shard_map/while/body/eval_jaxpr/gather | solution.py:52
  228.7 4.0 %copy.35 = bf16[48,128,2,128]{3,1,0,2:T(8,128)(2,1)} copy(bf16[48,128,2,128]{3,1,2,0:T(8,128)(2,1)} %gather_fusion) | data formatting | bytes 6291456 | tf_op jit(solution)/shard_map/while/body/eval_jaxpr/gather | solution.py:52
  239.2 4.9 %gather_fusion = bf16[48,128,2,128]{3,1,2,0:T(8,128)(2,1)} fusion(bf16[64,128,2,128]{3,1,2,0:T(8,128)(2,1)} %bitcast.87, s32[1024]{0:T(1024)S(1)} %pad_clamp_fusion.2), kind=kCustom, calls=%fused_computation.clone.1 | custom fusion | bytes 6291648 | tf_op jit(solution)/shard_map/while/body/eval_jaxpr/gather | solution.py:52
  244.1 4.0 %copy.35 = bf16[48,128,2,128]{3,1,0,2:T(8,128)(2,1)} copy(bf16[48,128,2,128]{3,1,2,0:T(8,128)(2,1)} %gather_fusion) | data formatting | bytes 6291456 | tf_op jit(solution)/shard_map/while/body/eval_jaxpr/gather | solution.py:52
  254.6 4.9 %gather_fusion = bf16[48,128,2,128]{3,1,2,0:T(8,128)(2,1)} fusion(bf16[64,128,2,128]{3,1,2,0:T(8,128)(2,1)} %bitcast.87, s32[1024]{0:T(1024)S(1)} %pad_clamp_fusion.2), kind=kCustom, calls=%fused_computation.clone.1 | custom fusion | bytes 6291648 | tf_op jit(solution)/shard_map/while/body/eval_jaxpr/gather | solution.py:52
  259.5 4.0 %copy.35 = bf16[48,128,2,128]{3,1,0,2:T(8,128)(2,1)} copy(bf16[48,128,2,128]{3,1,2,0:T(8,128)(2,1)} %gather_fusion) | data formatting | bytes 6291456 | tf_op jit(solution)/shard_map/while/body/eval_jaxpr/gather | solution.py:52
  270.1 4.9 %gather_fusion = bf16[48,128,2,128]{3,1,2,0:T(8,128)(2,1)} fusion(bf16[64,128,2,128]{3,1,2,0:T(8,128)(2,1)} %bitcast.87, s32[1024]{0:T(1024)S(1)} %pad_clamp_fusion.2), kind=kCustom, calls=%fused_computation.clone.1 | custom fusion | bytes 6291648 | tf_op jit(solution)/shard_map/while/body/eval_jaxpr/gather | solution.py:52
  275.0 4.0 %copy.35 = bf16[48,128,2,128]{3,1,0,2:T(8,128)(2,1)} copy(bf16[48,128,2,128]{3,1,2,0:T(8,128)(2,1)} %gather_fusion) | data formatting | bytes 6291456 | tf_op jit(solution)/shard_map/while/body/eval_jaxpr/gather | solution.py:52
  285.5 4.9 %gather_fusion = bf16[48,128,2,128]{3,1,2,0:T(8,128)(2,1)} fusion(bf16[64,128,2,128]{3,1,2,0:T(8,128)(2,1)} %bitcast.87, s32[1024]{0:T(1024)S(1)} %pad_clamp_fusion.2), kind=kCustom, calls=%fused_computation.clone.1 | custom fusion | bytes 6291648 | tf_op jit(solution)/shard_map/while/body/eval_jaxpr/gather | solution.py:52
  290.4 4.0 %copy.35 = bf16[48,128,2,128]{3,1,0,2:T(8,128)(2,1)} copy(bf16[48,128,2,128]{3,1,2,0:T(8,128)(2,1)} %gather_fusion) | data formatting | bytes 6291456 | tf_op jit(solution)/shard_map/while/body/eval_jaxpr/gather | solution.py:52
  300.9 4.9 %gather_fusion = bf16[48,128,2,128]{3,1,2,0:T(8,128)(2,1)} fusion(bf16[64,128,2,128]{3,1,2,0:T(8,128)(2,1)} %bitcast.87, s32[1024]{0:T(1024)S(1)} %pad_clamp_fusion.2), kind=kCustom, calls=%fused_computation.clone.1 | custom fusion | bytes 6291648 | tf_op jit(solution)/shard_map/while/body/eval_jaxpr/gather | solution.py:52
  305.9 4.0 %copy.35 = bf16[48,128,2,128]{3,1,0,2:T(8,128)(2,1)} copy(bf16[48,128,2,128]{3,1,2,0:T(8,128)(2,1)} %gather_fusion) | data formatting | bytes 6291456 | tf_op jit(solution)/shard_map/while/body/eval_jaxpr/gather | solution.py:52
  316.4 4.9 %gather_fusion = bf16[48,128,2,128]{3,1,2,0:T(8,128)(2,1)} fusion(bf16[64,128,2,128]{3,1,2,0:T(8,128)(2,1)} %bitcast.87, s32[1024]{0:T(1024)S(1)} %pad_clamp_fusion.2), kind=kCustom, calls=%fused_computation.clone.1 | custom fusion | bytes 6291648 | tf_op jit(solution)/shard_map/while/body/eval_jaxpr/gather | solution.py:52
  321.3 4.0 %copy.35 = bf16[48,128,2,128]{3,1,0,2:T(8,128)(2,1)} copy(bf16[48,128,2,128]{3,1,2,0:T(8,128)(2,1)} %gather_fusion) | data formatting | bytes 6291456 | tf_op jit(solution)/shard_map/while/body/eval_jaxpr/gather | solution.py:52
  334.0 32.8 %all_to_all.34 = bf16[8,2,32768]{2,1,0:T(2,128)(2,1)} all-to-all(bf16[8,2,32768]{2,1,0:T(2,128)(2,1)S(1)} %reshape.97), channel_id=1, replica_groups=mesh['seq'=32,'head'=8] {'head'}, dimensions={0} | all-to-all | bytes 2097152 | tf_op jit(solution)/shard_map/all_to_all | solution.py:68
  366.8 4.3 %reshape.98 = bf16[4096,1,128]{2,1,0:T(2,128)(2,1)S(1)} reshape(bf16[8,2,32768]{2,1,0:T(2,128)(2,1)} %all_to_all.34) | data formatting | bytes 2097152
  (86 shorter events, 76.2 us)
Async XLA Ops:
  6.5 71.9 %copy-start = (bf16[512,1024]{1,0:T(8,128)(2,1)S(1)}, bf16[512,1024]{1,0:T(8,128)(2,1)}, u32[]{:S(2)}) copy-start(bf16[512,1024]{1,0:T(8,128)(2,1)} %param.6) | copy-start | bytes 3145732
  6.5 71.9 %all-gather.3.cloned.1.call-start = ((), (), s32[]{:S(2)}) async-start(), calls=%async_computation.2 | async-start | bytes 6488064 | tf_op jit(solution)/shard_map/all_gather | solution.py:36
  7.3 366.5 %all-gather.5.cloned.1.call-start = ((), (), s32[]{:S(2)}) async-start(), calls=%async_computation.3 | async-start | bytes 2162688 | tf_op jit(solution)/shard_map/all_gather | solution.py:70
  169.1 1.7 copy-start.1
  169.1 5.2 %copy-start.2 = (s32[32,12]{0,1:T(8,128)S(1)}, s32[32,12]{0,1:T(8,128)}, u32[]{:S(2)}) copy-start(s32[32,12]{0,1:T(8,128)} %param.9) | copy-start | bytes 4612
  171.9 23.4 %collective-permute-start = (bf16[2048,2,1,128]{3,0,1,2:T(8,128)(2,1)}, bf16[2048,2,1,128]{3,0,1,2:T(8,128)(2,1)}, u32[]{:S(2)}, u32[]{:S(2)}) collective-permute-start(bf16[2048,2,1,128]{3,0,1,2:T(8,128)(2,1)} %get-tuple-element.53), channel_id=1, source_target_pairs={{0,8},{8,16},{16,24},{24,32},{32,40},{40,48},{48,56},{56,64},{64,7... | collective-permute-start | bytes 3145736 | tf_op jit(solution)/shard_map/ppermute | solution.py:21
  174.3 29.9 %collective-permute-start.1 = (bf16[2048,2,1,128]{3,0,1,2:T(8,128)(2,1)S(1)}, bf16[2048,2,1,128]{3,0,1,2:T(8,128)(2,1)}, u32[]{:S(2)}, u32[]{:S(2)}) collective-permute-start(bf16[2048,2,1,128]{3,0,1,2:T(8,128)(2,1)S(1)} %get-tuple-element.54), channel_id=1, source_target_pairs={{8,0},{16,8},{24,16},{32,24},{40,32},{48,40},{56,48},{64,56},{72,6... | collective-permute-start | bytes 3145736 | tf_op jit(solution)/shard_map/ppermute | solution.py:23
Sparse Core Ops, SparseCore 0:
  9.2 69.2 all-gather.2
  174.4 60.0 all-gather.4
where the time goes:
time: 386 us; the launch traced here: 384 us
  blocking collectives  115 us (30%)
  waiting for transfers between devices  97.6 us (25%)
  local copies, waits for them, and re-layouts  92.1 us (24%)
  matrix products  59.9 us (16%)
  between operations  13.5 us (3%)
    all_to_all x1, blocking collectives, local(): lax.all_to_all(projected, 'head', split_axis=2, concat_axis=0, tiled=True)  82.3 us
    gather x16, local copies, waits for them, and re-layouts, attend(): kv_blocks[list_group].reshape(group_blocks, NBR * BLK, 2, per_device, HD)  71.6 us
    all_gather x1, waiting for transfers between devices, local(): full_qkv = lax.all_gather(w_qkv, 'seq', axis=0, tiled=True)  71.2 us
    all_to_all x1, blocking collectives, local(): lax.all_to_all(attended, 'head', split_axis=0, concat_axis=1, tiled=True)  32.8 us
    dot_general x8, matrix products, attend(): jnp.einsum('nhqk,nkhd->nqhd', probs, values, preferred_element_type=jnp.f...  29.2 us
    sub x8, matrix products, attend(): expo = jnp.exp(scores - largest)  20.5 us
    ppermute x1, waiting for transfers between devices, padded_2(): lax.ppermute(tail, axis, [(i, (i + 1) % count) for i in range(count)])  16.8 us
    ppermute x1, waiting for transfers between devices, padded_2(): lax.ppermute(head, axis, [((i + 1) % count, i) for i in range(count)])  8.94 us
  transfers between devices with their start and end apart: 4, of which 3 were waited for; matrix products, arithmetic and copies ran while one was open for 37% of the time, Pallas kernels for 0%

commit v1 on v0

--- a/solution.py
+++ b/solution.py
@@ -36,7 +36,12 @@
     full_qkv = lax.all_gather(w_qkv, "seq", axis=0, tiled=True)
     projected = jnp.dot(tokens, full_qkv, preferred_element_type=jnp.float32)
     projected = projected.astype(jnp.bfloat16).reshape(local_rows, 3, HEADS, HD)
-    slab = lax.all_to_all(projected, "head", split_axis=2, concat_axis=0, tiled=True)
+    slab = jnp.concatenate(
+        lax.all_to_all(
+            jnp.stack(jnp.split(projected, lax.axis_size("head"), axis=2)), "head", 0, 0
+        ),
+        axis=0,
+    )
     queries = slab[:, 0]
     key_value = slab[:, 1:3]
     padded = padded_2(key_value, (("seq", 0),), PB * BLK)

time: 386 us -> 391 us (1.013)
  local copies, waits for them, and re-layouts: 92.1 us -> 97.8 us
    split x0 -> x1, local copies, waits for them, and re-layouts: none -> 5.72 us  [local(): jnp.split(projected, lax.axis_size('head'), axis=2)]
    unnamed x10 -> x17, local copies, waits for them, and re-layouts: 8.19 us -> 8.83 us
  transfers between devices with their start and end apart: 4 -> 4, of which waited for: 3 -> 3; matrix products, arithmetic and copies ran while one was open for 37% -> 36% of each run, Pallas kernels for 0% -> 0%
where the time goes in v1:
time: 391 us; the launch traced here: 390 us
  blocking collectives  115 us (29%)
  local copies, waits for them, and re-layouts  97.8 us (25%)
  waiting for transfers between devices  97.6 us (25%)
  matrix products  59.9 us (15%)
  between operations  13.6 us (3%)
    all_to_all x1, blocking collectives, local(): lax.all_to_all(jnp.stack(jnp.split(projected, lax.axis_size('head'), axis...  82.3 us
    gather x16, local copies, waits for them, and re-layouts, attend(): kv_blocks[list_group].reshape(group_blocks, NBR * BLK, 2, per_device, HD)  71.5 us
    all_gather x1, waiting for transfers between devices, local(): full_qkv = lax.all_gather(w_qkv, 'seq', axis=0, tiled=True)  71.2 us
    all_to_all x1, blocking collectives, local(): lax.all_to_all(attended, 'head', split_axis=0, concat_axis=1, tiled=True)  32.9 us
    dot_general x8, matrix products, attend(): jnp.einsum('nhqk,nkhd->nqhd', probs, values, preferred_element_type=jnp.f...  29.1 us
    sub x8, matrix products, attend(): expo = jnp.exp(scores - largest)  20.5 us
    ppermute x1, waiting for transfers between devices, padded_2(): lax.ppermute(tail, axis, [(i, (i + 1) % count) for i in range(count)])  16.7 us
    ppermute x1, waiting for transfers between devices, padded_2(): lax.ppermute(head, axis, [((i + 1) % count, i) for i in range(count)])  8.94 us
  transfers between devices with their start and end apart: 4, of which 3 were waited for; matrix products, arithmetic and copies ran while one was open for 36% of the time, Pallas kernels for 0%

profile of v1, /device:TPU:33, one launch (start us, length us, event | category | flops | bytes accessed | tf_op | source)
XLA Modules:
  0.0 390.2 jit_solution(3341953515791425075)
XLA Ops:
  7.3 71.2 %all-gather.3.cloned.1.call-done = bf16[1024,3072]{1,0:T(8,128)(2,1)} async-done(((bf16[32,3072]{1,0:T(8,128)(2,1)}), bf16[1024,3072]{1,0:T(8,128)(2,1)}) %all-gather.3.cloned.1.call-update) | async-done | bytes 6291472 | tf_op jit(solution)/shard_map/all_gather | solution.py:36
  78.5 6.4 %fusion.29 = bf16[64,8,24,128]{3,1,2,0:T(8,128)(2,1)S(1)} fusion(bf16[512,1024]{1,0:T(8,128)(2,1)S(1)} %copy-done, bf16[1024,3072]{1,0:T(8,128)(2,1)} %all-gather.3.cloned.1.call-done), kind=kOutput, calls=%fused_computation.27 | convolution fusion | flops 3222798336 | bytes 10485760 | tf_op jit(solution)/shard_map/dot_general | solution.py:37
  85.8 5.7 %fusion.43 = (bf16[512,3,1,128]{3,2,1,0:T(2,128)(2,1)S(1)}, bf16[512,3,1,128]{3,2,1,0:T(2,128)(2,1)S(1)}, bf16[512,3,1,128]{3,2,1,0:T(2,128)(2,1)S(1)}, bf16[512...) fusion(bf16[512,3,8,128]{3,2,1,0:T(8,128)(2,1)S(1)} %bitcast.118), kind=kLoop, calls=%fused_computation.51 | loop fusion | bytes 6291456 | tf_op jit(solution)/shard_map/split | solution.py:41
  92.3 82.3 %all_to_all.20 = bf16[8,512,3,1,128]{4,1,3,2,0:T(8,128)(2,1)S(1)} all-to-all(bf16[8,512,3,1,128]{4,1,3,2,0:T(8,128)(2,1)S(1)} %fusion.30), channel_id=1, replica_groups=mesh['seq'=32,'head'=8] {'head'}, dimensions={0} | all-to-all | bytes 6291456 | tf_op jit(solution)/shard_map/all_to_all | solution.py:40
  184.4 16.7 %collective-permute-done = bf16[2048,2,1,128]{3,0,1,2:T(8,128)(2,1)} collective-permute-done((bf16[2048,2,1,128]{3,0,1,2:T(8,128)(2,1)}, bf16[2048,2,1,128]{3,0,1,2:T(8,128)(2,1)}, u32[]{:S(2)}, u32[]{:S(2)}) %collective-permute-start) | collective-permute-done | bytes 1048608 | tf_op jit(solution)/shard_map/ppermute | solution.py:21
  201.1 8.9 %collective-permute-done.1 = bf16[2048,2,1,128]{3,0,1,2:T(8,128)(2,1)} collective-permute-done((bf16[2048,2,1,128]{3,0,1,2:T(8,128)(2,1)S(1)}, bf16[2048,2,1,128]{3,0,1,2:T(8,128)(2,1)}, u32[]{:S(2)}, u32[]{:S(2)}) %collective-permute-start.1) | collective-permute-done | bytes 1048608 | tf_op jit(solution)/shard_map/ppermute | solution.py:23
  214.0 123.5 %while.10 = (s32[]{:T(128)}, bf16[8,4,128,1,128]{4,2,1,0,3:T(8,128)(2,1)S(1)}, s32[8,4,12]{2,1,0:T(4,128)S(1)}, bf16[64,128,2,1,128]{4,1,3,2,0:T(8,128)(2,1)}, bf16[8,4,128,1,128]{4,2,1,3,0:T(8,128)(2,1)}, /*index=5*/s32[]{:T(128)}) while((s32[]{:T(128)}, bf16[8,4,128,1,128]{4,2,1,0,3:T(8,128)(2,1)S(1)}, s32[8,4,12]{2,1,0:T(4,128)S(1)}, ...), condition=%wide.region_3.4_spmd, body=%wide.region_0.3_spmd.sunk | while | flops 609555072 | bytes 18229452 | solution.py:72
  214.1 4.9 %gather_fusion = bf16[48,128,2,128]{3,1,2,0:T(8,128)(2,1)} fusion(bf16[64,128,2,128]{3,1,2,0:T(8,128)(2,1)} %bitcast.115, s32[1024]{0:T(1024)S(1)} %pad_clamp_fusion.2), kind=kCustom, calls=%fused_computation.clone.1 | custom fusion | bytes 6291648 | tf_op jit(solution)/shard_map/while/body/eval_jaxpr/gather | solution.py:57
  219.0 4.0 %copy.104 = bf16[48,128,2,128]{3,1,0,2:T(8,128)(2,1)} copy(bf16[48,128,2,128]{3,1,2,0:T(8,128)(2,1)} %gather_fusion) | data formatting | bytes 6291456 | tf_op jit(solution)/shard_map/while/body/eval_jaxpr/gather | solution.py:57
  229.6 4.9 %gather_fusion = bf16[48,128,2,128]{3,1,2,0:T(8,128)(2,1)} fusion(bf16[64,128,2,128]{3,1,2,0:T(8,128)(2,1)} %bitcast.115, s32[1024]{0:T(1024)S(1)} %pad_clamp_fusion.2), kind=kCustom, calls=%fused_computation.clone.1 | custom fusion | bytes 6291648 | tf_op jit(solution)/shard_map/while/body/eval_jaxpr/gather | solution.py:57
  245.0 4.9 %gather_fusion = bf16[48,128,2,128]{3,1,2,0:T(8,128)(2,1)} fusion(bf16[64,128,2,128]{3,1,2,0:T(8,128)(2,1)} %bitcast.115, s32[1024]{0:T(1024)S(1)} %pad_clamp_fusion.2), kind=kCustom, calls=%fused_computation.clone.1 | custom fusion | bytes 6291648 | tf_op jit(solution)/shard_map/while/body/eval_jaxpr/gather | solution.py:57
  249.9 4.0 %copy.104 = bf16[48,128,2,128]{3,1,0,2:T(8,128)(2,1)} copy(bf16[48,128,2,128]{3,1,2,0:T(8,128)(2,1)} %gather_fusion) | data formatting | bytes 6291456 | tf_op jit(solution)/shard_map/while/body/eval_jaxpr/gather | solution.py:57
  260.4 4.9 %gather_fusion = bf16[48,128,2,128]{3,1,2,0:T(8,128)(2,1)} fusion(bf16[64,128,2,128]{3,1,2,0:T(8,128)(2,1)} %bitcast.115, s32[1024]{0:T(1024)S(1)} %pad_clamp_fusion.2), kind=kCustom, calls=%fused_computation.clone.1 | custom fusion | bytes 6291648 | tf_op jit(solution)/shard_map/while/body/eval_jaxpr/gather | solution.py:57
  265.4 4.0 %copy.104 = bf16[48,128,2,128]{3,1,0,2:T(8,128)(2,1)} copy(bf16[48,128,2,128]{3,1,2,0:T(8,128)(2,1)} %gather_fusion) | data formatting | bytes 6291456 | tf_op jit(solution)/shard_map/while/body/eval_jaxpr/gather | solution.py:57
  275.9 4.9 %gather_fusion = bf16[48,128,2,128]{3,1,2,0:T(8,128)(2,1)} fusion(bf16[64,128,2,128]{3,1,2,0:T(8,128)(2,1)} %bitcast.115, s32[1024]{0:T(1024)S(1)} %pad_clamp_fusion.2), kind=kCustom, calls=%fused_computation.clone.1 | custom fusion | bytes 6291648 | tf_op jit(solution)/shard_map/while/body/eval_jaxpr/gather | solution.py:57
  280.8 4.0 %copy.104 = bf16[48,128,2,128]{3,1,0,2:T(8,128)(2,1)} copy(bf16[48,128,2,128]{3,1,2,0:T(8,128)(2,1)} %gather_fusion) | data formatting | bytes 6291456 | tf_op jit(solution)/shard_map/while/body/eval_jaxpr/gather | solution.py:57
  291.3 4.9 %gather_fusion = bf16[48,128,2,128]{3,1,2,0:T(8,128)(2,1)} fusion(bf16[64,128,2,128]{3,1,2,0:T(8,128)(2,1)} %bitcast.115, s32[1024]{0:T(1024)S(1)} %pad_clamp_fusion.2), kind=kCustom, calls=%fused_computation.clone.1 | custom fusion | bytes 6291648 | tf_op jit(solution)/shard_map/while/body/eval_jaxpr/gather | solution.py:57
  296.2 4.0 %copy.104 = bf16[48,128,2,128]{3,1,0,2:T(8,128)(2,1)} copy(bf16[48,128,2,128]{3,1,2,0:T(8,128)(2,1)} %gather_fusion) | data formatting | bytes 6291456 | tf_op jit(solution)/shard_map/while/body/eval_jaxpr/gather | solution.py:57
  306.7 4.9 %gather_fusion = bf16[48,128,2,128]{3,1,2,0:T(8,128)(2,1)} fusion(bf16[64,128,2,128]{3,1,2,0:T(8,128)(2,1)} %bitcast.115, s32[1024]{0:T(1024)S(1)} %pad_clamp_fusion.2), kind=kCustom, calls=%fused_computation.clone.1 | custom fusion | bytes 6291648 | tf_op jit(solution)/shard_map/while/body/eval_jaxpr/gather | solution.py:57
  311.7 4.0 %copy.104 = bf16[48,128,2,128]{3,1,0,2:T(8,128)(2,1)} copy(bf16[48,128,2,128]{3,1,2,0:T(8,128)(2,1)} %gather_fusion) | data formatting | bytes 6291456 | tf_op jit(solution)/shard_map/while/body/eval_jaxpr/gather | solution.py:57
  322.2 4.9 %gather_fusion = bf16[48,128,2,128]{3,1,2,0:T(8,128)(2,1)} fusion(bf16[64,128,2,128]{3,1,2,0:T(8,128)(2,1)} %bitcast.115, s32[1024]{0:T(1024)S(1)} %pad_clamp_fusion.2), kind=kCustom, calls=%fused_computation.clone.1 | custom fusion | bytes 6291648 | tf_op jit(solution)/shard_map/while/body/eval_jaxpr/gather | solution.py:57
  327.1 4.0 %copy.104 = bf16[48,128,2,128]{3,1,0,2:T(8,128)(2,1)} copy(bf16[48,128,2,128]{3,1,2,0:T(8,128)(2,1)} %gather_fusion) | data formatting | bytes 6291456 | tf_op jit(solution)/shard_map/while/body/eval_jaxpr/gather | solution.py:57
  339.7 32.9 %all_to_all.21 = bf16[8,2,32768]{2,1,0:T(2,128)(2,1)} all-to-all(bf16[8,2,32768]{2,1,0:T(2,128)(2,1)S(1)} %reshape.101), channel_id=1, replica_groups=mesh['seq'=32,'head'=8] {'head'}, dimensions={0} | all-to-all | bytes 2097152 | tf_op jit(solution)/shard_map/all_to_all | solution.py:73
  372.6 4.3 %reshape.102 = bf16[4096,1,128]{2,1,0:T(2,128)(2,1)S(1)} reshape(bf16[8,2,32768]{2,1,0:T(2,128)(2,1)} %all_to_all.21) | data formatting | bytes 2097152
  (94 shorter events, 80.3 us)
Async XLA Ops:
  6.5 71.9 %copy-start = (bf16[512,1024]{1,0:T(8,128)(2,1)S(1)}, bf16[512,1024]{1,0:T(8,128)(2,1)}, u32[]{:S(2)}) copy-start(bf16[512,1024]{1,0:T(8,128)(2,1)} %param.6) | copy-start | bytes 3145732
  6.5 71.9 %all-gather.3.cloned.1.call-start = ((), (), s32[]{:S(2)}) async-start(), calls=%async_computation.2 | async-start | bytes 6488064 | tf_op jit(solution)/shard_map/all_gather | solution.py:36
  7.3 372.3 %all-gather.5.cloned.1.call-start = ((), (), s32[]{:S(2)}) async-start(), calls=%async_computation.3 | async-start | bytes 2162688 | tf_op jit(solution)/shard_map/all_gather | solution.py:75
  175.0 1.7 copy-start.1
  175.0 5.2 %copy-start.2 = (s32[32,12]{0,1:T(8,128)S(1)}, s32[32,12]{0,1:T(8,128)}, u32[]{:S(2)}) copy-start(s32[32,12]{0,1:T(8,128)} %param.9) | copy-start | bytes 4612
  177.7 23.4 %collective-permute-start = (bf16[2048,2,1,128]{3,0,1,2:T(8,128)(2,1)}, bf16[2048,2,1,128]{3,0,1,2:T(8,128)(2,1)}, u32[]{:S(2)}, u32[]{:S(2)}) collective-permute-start(bf16[2048,2,1,128]{3,0,1,2:T(8,128)(2,1)} %get-tuple-element.58), channel_id=1, source_target_pairs={{0,8},{8,16},{16,24},{24,32},{32,40},{40,48},{48,56},{56,64},{64,7... | collective-permute-start | bytes 3145736 | tf_op jit(solution)/shard_map/ppermute | solution.py:21
  180.1 29.9 %collective-permute-start.1 = (bf16[2048,2,1,128]{3,0,1,2:T(8,128)(2,1)S(1)}, bf16[2048,2,1,128]{3,0,1,2:T(8,128)(2,1)}, u32[]{:S(2)}, u32[]{:S(2)}) collective-permute-start(bf16[2048,2,1,128]{3,0,1,2:T(8,128)(2,1)S(1)} %get-tuple-element.59), channel_id=1, source_target_pairs={{8,0},{16,8},{24,16},{32,24},{40,32},{48,40},{56,48},{64,56},{72,6... | collective-permute-start | bytes 3145736 | tf_op jit(solution)/shard_map/ppermute | solution.py:23
Sparse Core Ops, SparseCore 0:
  9.2 69.2 all-gather.2
  180.3 60.0 all-gather.4
